TPU v7x, 512 devices: a whole 4x4x16 slice. The times are simulated.
512 devices in a mesh: dp: 32 (over z, core), member: 16 (over y, x).
Axes of the slice: x: 4, y: 4, z: 16, core: 2. Of those that a mesh axis runs over, the one named last changes fastest.
Arguments:
- tokens: bfloat16 [4096, 4096], P('dp', 'member'), may hold values from -6 to 6
- routes: int32 [4096, 2], P('dp'), may hold values from 0 to 7, all different within a row; in each aligned block of 128 rows (0 to 127, 128 to 255, ...) at most 34 rows name the same one
- route_weights: float32 [4096, 2], P('dp'), may hold values from 0.2 to 1
- up_stacked: bfloat16 [8, 4096, 7168], P(None, ('member', 'dp')), may hold values from -0.09375 to 0.09375
- down_stacked: bfloat16 [8, 4096, 7168], P(None, ('member', 'dp')), may hold values from -0.0625 to 0.0625
- cotangent: bfloat16 [4096, 4096], P('dp', 'member'), may hold values from -6 to 6
Outputs:
- mixed: bfloat16 [4096, 4096], P('dp', 'member')
- grad_tokens: bfloat16 [4096, 4096], P('dp', 'member')
- grad_up: bfloat16 [32, 4096, 1792], P('dp', 'member')
- grad_down: bfloat16 [32, 4096, 1792], P('dp', 'member')
Inputs may be any that keep to these rules, and one draw needn't show every extreme that they name: `routes`: each row names two different experts. In each aligned block of 128 rows no expert is named by more than 34 rows, and in some block some expert is named by exactly 34 rows.
All inputs are finite; a program needn't handle non-finite values.
Results may differ from a plain program's by a relative error of at most 0.018.
Values may be sent and summed in bfloat16 or wider, within the bound.
A program may use at most 64 MiB of HBM per device.

v0:
```python
import jax
import jax.numpy as jnp
from jax import lax
from jax.sharding import PartitionSpec as P

FF_W = 7168
E = 8
CAP = 34


def contract(left, right, left_dim, right_dim):
    return lax.dot_general(
        left, right, (((left_dim,), (right_dim,)), ((), ())), preferred_element_type=jnp.float32
    )


def body(tokens, routes, route_weights, up_stacked, down_stacked, cotangent):
    dp_count = lax.axis_size("dp")
    member_count = lax.axis_size("member")
    quarters = dp_count // E
    share_rows = up_stacked.shape[1]
    features = tokens.shape[1]
    hidden_own = FF_W // quarters
    per_member = hidden_own // member_count
    slots_all = E * CAP
    up_parts = (
        up_stacked.reshape(E, share_rows, quarters, hidden_own)
        .transpose(0, 2, 1, 3)
        .reshape(dp_count, share_rows, hidden_own)
    )
    down_parts = (
        down_stacked.reshape(E, share_rows, quarters, hidden_own)
        .transpose(0, 2, 1, 3)
        .reshape(dp_count, share_rows, hidden_own)
    )
    up_own, down_own = (
        lax.all_to_all(up_parts, "dp", split_axis=0, concat_axis=1, tiled=True),
        lax.all_to_all(down_parts, "dp", split_axis=0, concat_axis=1, tiled=True),
    )
    up_own = up_own.reshape(dp_count * share_rows, hidden_own)
    down_own = down_own.reshape(dp_count * share_rows, hidden_own)
    chosen = (routes[:, :, None] == jnp.arange(E, dtype=jnp.int32)[None, None, :]).astype(jnp.int32)
    flat_hits = chosen.reshape(-1, E)
    before = jnp.cumsum(flat_hits, axis=0) - flat_hits
    slot_pos = jnp.sum(before * flat_hits, axis=1).reshape(-1, 2)
    target = routes * CAP + slot_pos
    slot_hits = jnp.arange(slots_all, dtype=jnp.int32)[:, None, None] == target[None, :, :]
    pick_table = jnp.sum(slot_hits.astype(jnp.float32), axis=2)
    weighted = jnp.sum(jnp.where(slot_hits, route_weights[None, :, :], 0.0), axis=2)
    x_local = jnp.dot(
        pick_table.astype(jnp.bfloat16), tokens, preferred_element_type=jnp.float32
    ).astype(jnp.bfloat16)
    d_local = jnp.dot(
        weighted, cotangent.astype(jnp.float32), precision=lax.Precision.HIGHEST
    ).astype(jnp.bfloat16)

    def spread(local):
        return jnp.broadcast_to(
            local.reshape(E, 1, CAP, features), (E, quarters, CAP, features)
        ).reshape(dp_count, CAP, features)

    def collect(returned):
        return jnp.sum(returned.reshape(E, quarters, CAP, features), axis=1).reshape(
            slots_all, features
        )

    x_in = lax.all_to_all(spread(x_local), "dp", split_axis=0, concat_axis=0, tiled=True).reshape(
        dp_count * CAP, features
    )
    partial_value = jnp.dot(x_in, up_own, preferred_element_type=jnp.float32).astype(jnp.bfloat16)
    pre_full = lax.psum(partial_value, "member").astype(jnp.float32)
    act_full = jax.nn.silu(pre_full).astype(jnp.bfloat16)
    y_part = contract(act_full, down_own, 1, 1)
    y_part, pre_full, act_full = (y_part, pre_full, act_full)
    y_back = lax.all_to_all(
        y_part.reshape(dp_count, CAP, features).astype(jnp.bfloat16),
        "dp",
        split_axis=0,
        concat_axis=0,
        tiled=True,
    ).astype(jnp.float32)
    d_in = lax.all_to_all(spread(d_local), "dp", split_axis=0, concat_axis=0, tiled=True).reshape(
        dp_count * CAP, features
    )
    d_act = lax.psum_scatter(
        contract(down_own, d_in, 0, 1).astype(jnp.bfloat16),
        "member",
        scatter_dimension=0,
        tiled=True,
    ).astype(jnp.float32)
    own_start = lax.axis_index("member") * per_member
    pre_share = lax.dynamic_slice_in_dim(pre_full, own_start, per_member, 1).T
    sigma = jax.nn.sigmoid(pre_share)
    d_share = (d_act * sigma * (1.0 + pre_share * (1.0 - sigma))).astype(jnp.bfloat16)
    d_pre = lax.all_gather(d_share, "member", axis=0, tiled=True)
    g_down = contract(d_in, act_full, 0, 0)
    g_up = contract(x_in, d_pre, 0, 1)
    dx_part = contract(d_pre, up_own, 0, 1)
    dx_part, g_up, g_down = (dx_part, g_up, g_down)
    dx_back = lax.all_to_all(
        dx_part.reshape(dp_count, CAP, features).astype(jnp.bfloat16),
        "dp",
        split_axis=0,
        concat_axis=0,
        tiled=True,
    ).astype(jnp.float32)
    y_slots = collect(y_back)
    dx_slots = collect(dx_back)
    mixed = jnp.dot(weighted.T, y_slots, precision=lax.Precision.HIGHEST).astype(jnp.bfloat16)
    grad_tokens = jnp.dot(pick_table.T, dx_slots, precision=lax.Precision.HIGHEST).astype(
        jnp.bfloat16
    )
    grad_up = g_up.astype(jnp.bfloat16).reshape(1, features, hidden_own)
    grad_down = g_down.astype(jnp.bfloat16).reshape(1, features, hidden_own)
    return (mixed, grad_tokens, grad_up, grad_down)


def solution(mesh):
    placed = (
        P("dp", "member"),
        P("dp", None),
        P("dp", None),
        P(None, ("member", "dp"), None),
        P(None, ("member", "dp"), None),
        P("dp", "member"),
    )
    return jax.shard_map(
        body,
        mesh=mesh,
        in_specs=placed,
        out_specs=(
            P("dp", "member"),
            P("dp", "member"),
            P("dp", "member", None),
            P("dp", "member", None),
        ),
        check_vma=False,
    )
```

profile of v0, /device:TPU:1, one launch (start us, length us, event | category | flops | bytes accessed | tf_op | source)
XLA Modules:
  0.0 533.8 jit_solution(7201500621114122409)
XLA Ops:
  7.2 0.8 copy.35
  8.1 0.1 eq.40
  8.3 0.6 reduce-window.6
  8.9 0.2 slice_reduce_fusion
  9.2 0.1 reshape.98
  9.4 0.7 multiply_add_fusion
  10.1 0.8 convert_reduce_fusion.2
  10.9 0.3 convolution_convert_fusion.6
  11.2 0.9 broadcast_in_dim.36
  12.1 16.8 %all-to-all-start.4 = ((bf16[32,34,256]{2,1,0:T(8,128)(2,1)}), bf16[32,34,256]{2,1,0:T(8,128)(2,1)S(1)}, u32[]{:S(2)}, u32[]{:S(2)}) async-start(bf16[32,34,256]{2,1,0:T(8,128)(2,1)} %bitcast.9), calls=%async_computation.4 | async-start | bytes 1310720 | tf_op jit(solution)/shard_map/all_to_all | solution.py:82
  28.9 1.0 convolution_convert_fusion.7
  30.0 38.0 %all-to-all-done.4 = bf16[32,34,256]{2,1,0:T(8,128)(2,1)S(1)} async-done(((bf16[32,34,256]{2,1,0:T(8,128)(2,1)}), bf16[32,34,256]{2,1,0:T(8,128)(2,1)S(1)}, u32[]{:S(2)}, u32[]{:S(2)}) %all-to-all-start.4) | async-done | bytes 557088 | tf_op jit(solution)/shard_map/all_to_all | solution.py:82
  68.0 0.9 broadcast_in_dim.34
  68.8 4.1 all-to-all-start
  72.9 1.3 fusion.16
  74.3 1.0 pad_maximum_fusion.1
  75.3 36.7 %all-to-all-done = bf16[32,34,256]{2,1,0:T(8,128)(2,1)S(1)} async-done(((bf16[32,34,256]{2,1,0:T(8,128)(2,1)}), bf16[32,34,256]{2,1,0:T(8,128)(2,1)S(1)}, u32[]{:S(2)}, u32[]{:S(2)}) %all-to-all-start) | async-done | bytes 557088 | tf_op jit(solution)/shard_map/all_to_all | solution.py:67
  112.0 0.8 copy-done.2
  112.8 4.5 all-to-all-start.2
  117.3 1.3 fusion.17
  118.7 1.0 pad_maximum_fusion
  119.7 47.9 %all-to-all-done.2 = bf16[32,8,1792]{2,1,0:T(8,128)(2,1)S(1)} async-done(((bf16[32,8,1792]{2,1,0:T(8,128)(2,1)}), bf16[32,8,1792]{2,1,0:T(8,128)(2,1)S(1)}, u32[]{:S(2)}, u32[]{:S(2)}) %all-to-all-start.2) | async-done | bytes 917536 | tf_op jit(solution)/shard_map/all_to_all | solution.py:38
  167.6 4.5 all-to-all-start.1
  172.2 1.0 reshape.109
  173.1 1.3 reshape.100
  174.4 4.4 convolution_convert_fusion
  178.8 6.4 %copy.38 = bf16[1792,1088]{0,1:T(8,128)(2,1)} copy(bf16[1792,1088]{1,0:T(8,128)(2,1)} %convolution_convert_fusion) | data formatting | bytes 7798784 | tf_op jit(solution)/shard_map/convert_element_type | solution.py:86
  185.2 37.2 %all-to-all-done.1 = bf16[32,8,1792]{2,1,0:T(8,128)(2,1)S(1)} async-done(((bf16[32,8,1792]{2,1,0:T(8,128)(2,1)}), bf16[32,8,1792]{2,1,0:T(8,128)(2,1)S(1)}, u32[]{:S(2)}, u32[]{:S(2)}) %all-to-all-start.1) | async-done | bytes 917536 | tf_op jit(solution)/shard_map/all_to_all | solution.py:37
  222.4 3.1 convolution_convert_fusion.1
  225.6 1.3 dynamic-slice
  227.5 156.5 %all-reduce.4.cloned.1.call-done = (bf16[1088,1792]{1,0:T(8,128)(2,1)}, bf16[1792,1088]{0,1:T(8,128)(2,1)}) async-done(((bf16[1088,1792]{1,0:T(8,128)(2,1)}, bf16[1792,1088]{0,1:T(8,128)(2,1)}), (bf16[1088,1792]{1,0:T(8,128)(2,1)}, bf16[1792,1088]{0,1:T(8,128)(2,1)})) %all-reduce.4.cloned.1.call-update) | async-done | bytes 7798800 | tf_op jit(solution)/shard_map/psum | solution.py:71
  384.0 2.7 convert_element_type.65
  386.7 1.4 fusion.11
  388.1 0.9 copy.39
  389.0 5.0 multiply_convert_fusion
  394.0 6.9 %dot_general.38 = bf16[32,34,1792]{2,1,0:T(8,128)(2,1)} reshape(bf16[1088,1792]{1,0:T(8,128)(2,1)} %multiply_convert_fusion) | data formatting | bytes 7798784 | tf_op jit(solution)/shard_map/dot_general | solution.py:12
  400.9 4.6 convolution_convert_fusion.5
  405.5 13.0 %all-to-all-start.3 = ((bf16[32,34,256]{2,1,0:T(8,128)(2,1)}), bf16[32,34,256]{2,1,0:T(8,128)(2,1)S(1)}, u32[]{:S(2)}, u32[]{:S(2)}) async-start(bf16[32,34,256]{2,1,0:T(8,128)(2,1)} %convolution_convert_fusion.5), calls=%async_computation.3 | async-start | bytes 1310720 | tf_op jit(solution)/shard_map/all_to_all | solution.py:75
  418.5 37.1 %all-gather.2.cloned.1.call-done = bf16[1792,1088]{1,0:T(8,128)(2,1)} async-done(((bf16[112,1088]{1,0:T(8,128)(2,1)}), bf16[1792,1088]{1,0:T(8,128)(2,1)}) %all-gather.2.cloned.1.call-update) | async-done | bytes 3899408 | tf_op jit(solution)/shard_map/all_gather | solution.py:95
  455.6 6.4 %copy.40 = bf16[1088,1792]{1,0:T(8,128)(2,1)} copy(bf16[1088,1792]{0,1:T(8,128)(2,1)} %bitcast.72) | data formatting | bytes 7798784 | tf_op jit(solution)/shard_map/dot_general | solution.py:12
  462.0 6.9 %dot_general.44 = bf16[32,34,1792]{2,1,0:T(8,128)(2,1)} reshape(bf16[1088,1792]{1,0:T(8,128)(2,1)} %copy.40) | data formatting | bytes 7798784 | tf_op jit(solution)/shard_map/dot_general | solution.py:12
  468.9 4.7 convolution_convert_fusion.4
  473.6 13.0 %all-to-all-start.5 = ((bf16[32,34,256]{2,1,0:T(8,128)(2,1)}), bf16[32,34,256]{2,1,0:T(8,128)(2,1)S(1)}, u32[]{:S(2)}, u32[]{:S(2)}) async-start(bf16[32,34,256]{2,1,0:T(8,128)(2,1)} %convolution_convert_fusion.4), calls=%async_computation.5 | async-start | bytes 1310720 | tf_op jit(solution)/shard_map/all_to_all | solution.py:100
  486.6 4.4 fusion.1
  491.2 1.1 convolution_convert_fusion.9
  492.3 4.5 fusion
  496.8 28.9 %all-to-all-done.5 = bf16[32,34,256]{2,1,0:T(8,128)(2,1)S(1)} async-done(((bf16[32,34,256]{2,1,0:T(8,128)(2,1)}), bf16[32,34,256]{2,1,0:T(8,128)(2,1)S(1)}, u32[]{:S(2)}, u32[]{:S(2)}) %all-to-all-start.5) | async-done | bytes 557088 | tf_op jit(solution)/shard_map/all_to_all | solution.py:100
  525.8 1.1 convolution_convert_fusion.8
  (24 shorter events, 0.8 us)
Async XLA Ops:
  7.2 3.7 copy-start
  12.1 55.9 %all-to-all-start.4 = ((bf16[32,34,256]{2,1,0:T(8,128)(2,1)}), bf16[32,34,256]{2,1,0:T(8,128)(2,1)S(1)}, u32[]{:S(2)}, u32[]{:S(2)}) async-start(bf16[32,34,256]{2,1,0:T(8,128)(2,1)} %bitcast.9), calls=%async_computation.4 | async-start | bytes 1310720 | tf_op jit(solution)/shard_map/all_to_all | solution.py:82
  68.8 43.1 %all-to-all-start = ((bf16[32,34,256]{2,1,0:T(8,128)(2,1)}), bf16[32,34,256]{2,1,0:T(8,128)(2,1)S(1)}, u32[]{:S(2)}, u32[]{:S(2)}) async-start(bf16[32,34,256]{2,1,0:T(8,128)(2,1)} %bitcast.2), calls=%async_computation | async-start | bytes 1310720 | tf_op jit(solution)/shard_map/all_to_all | solution.py:67
  112.0 0.8 copy-start.2
  112.8 54.7 %all-to-all-start.2 = ((bf16[32,8,1792]{2,1,0:T(8,128)(2,1)}), bf16[32,8,1792]{2,1,0:T(8,128)(2,1)S(1)}, u32[]{:S(2)}, u32[]{:S(2)}) async-start(bf16[32,8,1792]{2,1,0:T(8,128)(2,1)} %bitcast.5), calls=%async_computation.2 | async-start | bytes 1835008 | tf_op jit(solution)/shard_map/all_to_all | solution.py:38
  167.6 54.8 %all-to-all-start.1 = ((bf16[32,8,1792]{2,1,0:T(8,128)(2,1)}), bf16[32,8,1792]{2,1,0:T(8,128)(2,1)S(1)}, u32[]{:S(2)}, u32[]{:S(2)}) async-start(bf16[32,8,1792]{2,1,0:T(8,128)(2,1)} %bitcast.3), calls=%async_computation.1 | async-start | bytes 1835008 | tf_op jit(solution)/shard_map/all_to_all | solution.py:37
  172.1 211.8 %all-reduce.4.cloned.1.call-start = ((), (), s32[]{:S(2)}) async-start(), calls=%async_computation.7 | async-start | bytes 15597568 | tf_op jit(solution)/shard_map/psum | solution.py:71
  225.5 230.1 %all-gather.2.cloned.1.call-start = ((), (), s32[]{:S(2)}) async-start(), calls=%async_computation.6 | async-start | bytes 4386816 | tf_op jit(solution)/shard_map/all_gather | solution.py:95
  405.5 68.1 %all-to-all-start.3 = ((bf16[32,34,256]{2,1,0:T(8,128)(2,1)}), bf16[32,34,256]{2,1,0:T(8,128)(2,1)S(1)}, u32[]{:S(2)}, u32[]{:S(2)}) async-start(bf16[32,34,256]{2,1,0:T(8,128)(2,1)} %convolution_convert_fusion.5), calls=%async_computation.3 | async-start | bytes 1310720 | tf_op jit(solution)/shard_map/all_to_all | solution.py:75
  468.9 17.7 %copy-start.3 = (bf16[1088,256]{1,0:T(8,128)(2,1)S(1)}, bf16[1088,256]{1,0:T(8,128)(2,1)}, u32[]{:S(2)}) copy-start(bf16[1088,256]{1,0:T(8,128)(2,1)} %reshape.109) | copy-start | bytes 1671172
  473.6 52.1 %all-to-all-start.5 = ((bf16[32,34,256]{2,1,0:T(8,128)(2,1)}), bf16[32,34,256]{2,1,0:T(8,128)(2,1)S(1)}, u32[]{:S(2)}, u32[]{:S(2)}) async-start(bf16[32,34,256]{2,1,0:T(8,128)(2,1)} %convolution_convert_fusion.4), calls=%async_computation.5 | async-start | bytes 1310720 | tf_op jit(solution)/shard_map/all_to_all | solution.py:100
  491.2 35.8 %copy-start.1 = (bf16[128,256]{1,0:T(8,128)(2,1)S(1)}, bf16[128,256]{1,0:T(8,128)(2,1)}, u32[]{:S(2)}) copy-start(bf16[128,256]{1,0:T(8,128)(2,1)} %param.11) | copy-start | bytes 196612
Sparse Core Ops, SparseCore 0:
  225.7 158.2 all-reduce.3
  389.1 66.4 all-gather.1
where the time goes:
time: 535 us; the launch traced here: 534 us
  waiting for transfers between devices  382 us (71%)
  starting transfers between devices  55.9 us (10%)
  local copies, waits for them, and re-layouts  38 us (7%)
  matrix products  29.2 us (5%)
  between operations  14.9 us (3%)
  other arithmetic  13.5 us (3%)
    psum x1, waiting for transfers between devices, body(): pre_full = lax.psum(partial_value, 'member').astype(jnp.float32)  156 us
    all_to_all x1, waiting for transfers between devices, body(): lax.all_to_all(down_parts, 'dp', split_axis=0, concat_axis=1, tiled=True)  47.9 us
    all_to_all x1, waiting for transfers between devices, body(): lax.all_to_all(spread(d_local), 'dp', split_axis=0, concat_axis=0, tiled=...  38 us
    all_to_all x1, waiting for transfers between devices, body(): lax.all_to_all(up_parts, 'dp', split_axis=0, concat_axis=1, tiled=True)  37.2 us
    all_gather x1, waiting for transfers between devices, body(): d_pre = lax.all_gather(d_share, 'member', axis=0, tiled=True)  37.1 us
    all_to_all x1, waiting for transfers between devices, body(): lax.all_to_all(spread(x_local), 'dp', split_axis=0, concat_axis=0, tiled=...  36.7 us
    all_to_all x1, waiting for transfers between devices, body(): lax.all_to_all(dx_part.reshape(dp_count, CAP, features).astype(jnp.bfloat...  28.9 us
    dot_general x5, matrix products, contract(): lax.dot_general(left, right, (((left_dim,), (right_dim,)), ((), ())), pre...  22.5 us
  transfers between devices with their start and end apart: 8, of which 7 were waited for; matrix products, arithmetic and copies ran while one was open for 12% of the time, Pallas kernels for 0%

commit v1 on v0

--- a/solution.py
+++ b/solution.py
@@ -92,7 +92,9 @@
     pre_share = lax.dynamic_slice_in_dim(pre_full, own_start, per_member, 1).T
     sigma = jax.nn.sigmoid(pre_share)
     d_share = (d_act * sigma * (1.0 + pre_share * (1.0 - sigma))).astype(jnp.bfloat16)
-    d_pre = lax.all_gather(d_share, "member", axis=0, tiled=True)
+    d_pre = jnp.concatenate(
+        lax.all_to_all(jnp.stack([d_share] * lax.axis_size("member")), "member", 0, 0), axis=0
+    )
     g_down = contract(d_in, act_full, 0, 0)
     g_up = contract(x_in, d_pre, 0, 1)
     dx_part = contract(d_pre, up_own, 0, 1)

time: 535 us -> 563 us (1.052)
  waiting for transfers between devices: 382 us -> 411 us
    all_to_all x0 -> x1, waiting for transfers between devices: none -> 44.9 us  [body(): lax.all_to_all(jnp.stack([d_share] * lax.axis_size('member')), 'member',...]
    all_gather x1 -> x0, waiting for transfers between devices: 37.1 us -> none  [body(): d_pre = lax.all_gather(d_share, 'member', axis=0, tiled=True)]
    all_to_all x1, waiting for transfers between devices: 0.01 us -> 21 us  [body(): lax.all_to_all(y_part.reshape(dp_count, CAP, features).astype(jnp.bfloat1...]
    all_to_all x1, starting transfers between devices: 13 us -> 4.05 us  [body(): lax.all_to_all(dx_part.reshape(dp_count, CAP, features).astype(jnp.bfloat...]
  transfers between devices with their start and end apart: 8 -> 8, of which waited for: 7 -> 8; matrix products, arithmetic and copies ran while one was open for 12% -> 12% of each run, Pallas kernels for 0% -> 0%
where the time goes in v1:
time: 563 us; the launch traced here: 562 us
  waiting for transfers between devices  411 us (73%)
  starting transfers between devices  53.2 us (9%)
  local copies, waits for them, and re-layouts  39.6 us (7%)
  matrix products  29.2 us (5%)
  between operations  14.9 us (3%)
  other arithmetic  13.5 us (2%)
    psum x1, waiting for transfers between devices, body(): pre_full = lax.psum(partial_value, 'member').astype(jnp.float32)  156 us
    all_to_all x1, waiting for transfers between devices, body(): lax.all_to_all(down_parts, 'dp', split_axis=0, concat_axis=1, tiled=True)  47.9 us
    all_to_all x1, waiting for transfers between devices, body(): lax.all_to_all(jnp.stack([d_share] * lax.axis_size('member')), 'member',...  44.9 us
    all_to_all x1, waiting for transfers between devices, body(): lax.all_to_all(spread(d_local), 'dp', split_axis=0, concat_axis=0, tiled=...  38 us
    all_to_all x1, waiting for transfers between devices, body(): lax.all_to_all(up_parts, 'dp', split_axis=0, concat_axis=1, tiled=True)  37.1 us
    all_to_all x1, waiting for transfers between devices, body(): lax.all_to_all(spread(x_local), 'dp', split_axis=0, concat_axis=0, tiled=...  36.7 us
    all_to_all x1, waiting for transfers between devices, body(): lax.all_to_all(dx_part.reshape(dp_count, CAP, features).astype(jnp.bfloat...  28.8 us
    dot_general x5, matrix products, contract(): lax.dot_general(left, right, (((left_dim,), (right_dim,)), ((), ())), pre...  22.6 us
  transfers between devices with their start and end apart: 8, of which 8 were waited for; matrix products, arithmetic and copies ran while one was open for 12% of the time, Pallas kernels for 0%

profile of v1, /device:TPU:1, one launch (start us, length us, event | category | flops | bytes accessed | tf_op | source)
XLA Modules:
  0.0 561.6 jit_solution(6029290193083917425)
XLA Ops:
  7.2 0.8 copy.37
  8.3 0.6 reduce-window.6
  8.9 0.2 slice_reduce_fusion
  9.4 0.7 multiply_add_fusion
  10.1 0.8 convert_reduce_fusion.2
  10.9 0.3 convolution_convert_fusion.6
  11.2 0.9 broadcast_in_dim.36
  12.1 16.8 %all-to-all-start.4 = ((bf16[32,34,256]{2,1,0:T(8,128)(2,1)}), bf16[32,34,256]{2,1,0:T(8,128)(2,1)S(1)}, u32[]{:S(2)}, u32[]{:S(2)}) async-start(bf16[32,34,256]{2,1,0:T(8,128)(2,1)} %bitcast.9), calls=%async_computation.4 | async-start | bytes 1310720 | tf_op jit(solution)/shard_map/all_to_all | solution.py:82
  28.9 1.0 convolution_convert_fusion.7
  30.0 38.0 %all-to-all-done.4 = bf16[32,34,256]{2,1,0:T(8,128)(2,1)S(1)} async-done(((bf16[32,34,256]{2,1,0:T(8,128)(2,1)}), bf16[32,34,256]{2,1,0:T(8,128)(2,1)S(1)}, u32[]{:S(2)}, u32[]{:S(2)}) %all-to-all-start.4) | async-done | bytes 557088 | tf_op jit(solution)/shard_map/all_to_all | solution.py:82
  68.0 0.9 broadcast_in_dim.34
  68.8 4.1 all-to-all-start
  72.9 1.3 fusion.16
  74.3 1.0 pad_maximum_fusion.1
  75.3 36.7 %all-to-all-done = bf16[32,34,256]{2,1,0:T(8,128)(2,1)S(1)} async-done(((bf16[32,34,256]{2,1,0:T(8,128)(2,1)}), bf16[32,34,256]{2,1,0:T(8,128)(2,1)S(1)}, u32[]{:S(2)}, u32[]{:S(2)}) %all-to-all-start) | async-done | bytes 557088 | tf_op jit(solution)/shard_map/all_to_all | solution.py:67
  112.0 0.8 copy-done.2
  112.8 4.5 all-to-all-start.2
  117.3 1.3 fusion.17
  118.6 1.0 pad_maximum_fusion
  119.7 47.9 %all-to-all-done.2 = bf16[32,8,1792]{2,1,0:T(8,128)(2,1)S(1)} async-done(((bf16[32,8,1792]{2,1,0:T(8,128)(2,1)}), bf16[32,8,1792]{2,1,0:T(8,128)(2,1)S(1)}, u32[]{:S(2)}, u32[]{:S(2)}) %all-to-all-start.2) | async-done | bytes 917536 | tf_op jit(solution)/shard_map/all_to_all | solution.py:38
  167.6 4.5 all-to-all-start.1
  172.2 1.0 reshape.114
  173.1 1.3 reshape.105
  174.4 4.4 convolution_convert_fusion
  178.8 6.5 %copy.40 = bf16[1792,1088]{0,1:T(8,128)(2,1)} copy(bf16[1792,1088]{1,0:T(8,128)(2,1)} %convolution_convert_fusion) | data formatting | bytes 7798784 | tf_op jit(solution)/shard_map/convert_element_type | solution.py:86
  185.2 37.1 %all-to-all-done.1 = bf16[32,8,1792]{2,1,0:T(8,128)(2,1)S(1)} async-done(((bf16[32,8,1792]{2,1,0:T(8,128)(2,1)}), bf16[32,8,1792]{2,1,0:T(8,128)(2,1)S(1)}, u32[]{:S(2)}, u32[]{:S(2)}) %all-to-all-start.1) | async-done | bytes 917536 | tf_op jit(solution)/shard_map/all_to_all | solution.py:37
  222.4 3.1 convolution_convert_fusion.1
  225.5 1.3 dynamic-slice
  227.4 156.5 %all-reduce.4.cloned.1.call-done = (bf16[1088,1792]{1,0:T(8,128)(2,1)}, bf16[1792,1088]{0,1:T(8,128)(2,1)}) async-done(((bf16[1088,1792]{1,0:T(8,128)(2,1)}, bf16[1792,1088]{0,1:T(8,128)(2,1)}), (bf16[1088,1792]{1,0:T(8,128)(2,1)}, bf16[1792,1088]{0,1:T(8,128)(2,1)})) %all-reduce.4.cloned.1.call-update) | async-done | bytes 7798800 | tf_op jit(solution)/shard_map/psum | solution.py:71
  383.9 2.7 convert_element_type.65
  386.6 1.4 fusion.11
  388.2 2.2 stack.2
  390.5 5.1 all-to-all-start.5
  395.6 5.1 multiply_convert_fusion
  400.7 6.9 %dot_general.38 = bf16[32,34,1792]{2,1,0:T(8,128)(2,1)} reshape(bf16[1088,1792]{1,0:T(8,128)(2,1)} %multiply_convert_fusion) | data formatting | bytes 7798784 | tf_op jit(solution)/shard_map/dot_general | solution.py:12
  407.6 4.6 convolution_convert_fusion.5
  412.2 44.9 %all-to-all-done.5 = bf16[16,112,1088]{2,1,0:T(8,128)(2,1)} async-done(((bf16[16,112,1088]{2,1,0:T(8,128)(2,1)}), bf16[16,112,1088]{2,1,0:T(8,128)(2,1)}, u32[]{:S(2)}, u32[]{:S(2)}) %all-to-all-start.5) | async-done | bytes 3899424 | tf_op jit(solution)/shard_map/all_to_all | solution.py:96
  457.0 14.2 %all-to-all-start.3 = ((bf16[32,34,256]{2,1,0:T(8,128)(2,1)}), bf16[32,34,256]{2,1,0:T(8,128)(2,1)S(1)}, u32[]{:S(2)}, u32[]{:S(2)}) async-start(bf16[32,34,256]{2,1,0:T(8,128)(2,1)} %convolution_convert_fusion.5), calls=%async_computation.3 | async-start | bytes 1310720 | tf_op jit(solution)/shard_map/all_to_all | solution.py:75
  471.2 6.4 %copy.42 = bf16[1088,1792]{1,0:T(8,128)(2,1)} copy(bf16[1088,1792]{0,1:T(8,128)(2,1)} %bitcast.12) | data formatting | bytes 7798784 | tf_op jit(solution)/shard_map/dot_general | solution.py:12
  477.6 6.9 %dot_general.44 = bf16[32,34,1792]{2,1,0:T(8,128)(2,1)} reshape(bf16[1088,1792]{1,0:T(8,128)(2,1)} %copy.42) | data formatting | bytes 7798784 | tf_op jit(solution)/shard_map/dot_general | solution.py:12
  484.6 4.7 convolution_convert_fusion.4
  489.3 21.0 %all-to-all-done.3 = bf16[32,34,256]{2,1,0:T(8,128)(2,1)S(1)} async-done(((bf16[32,34,256]{2,1,0:T(8,128)(2,1)}), bf16[32,34,256]{2,1,0:T(8,128)(2,1)S(1)}, u32[]{:S(2)}, u32[]{:S(2)}) %all-to-all-start.3) | async-done | bytes 557088 | tf_op jit(solution)/shard_map/all_to_all | solution.py:75
  510.3 4.1 all-to-all-start.6
  514.4 4.4 fusion.1
  518.9 1.1 convolution_convert_fusion.9
  520.1 4.5 fusion
  524.6 28.8 %all-to-all-done.6 = bf16[32,34,256]{2,1,0:T(8,128)(2,1)S(1)} async-done(((bf16[32,34,256]{2,1,0:T(8,128)(2,1)}), bf16[32,34,256]{2,1,0:T(8,128)(2,1)S(1)}, u32[]{:S(2)}, u32[]{:S(2)}) %all-to-all-start.6) | async-done | bytes 557088 | tf_op jit(solution)/shard_map/all_to_all | solution.py:102
  553.6 1.1 convolution_convert_fusion.8
  (24 shorter events, 1.2 us)
Async XLA Ops:
  7.2 3.7 copy-start
  12.1 55.9 %all-to-all-start.4 = ((bf16[32,34,256]{2,1,0:T(8,128)(2,1)}), bf16[32,34,256]{2,1,0:T(8,128)(2,1)S(1)}, u32[]{:S(2)}, u32[]{:S(2)}) async-start(bf16[32,34,256]{2,1,0:T(8,128)(2,1)} %bitcast.9), calls=%async_computation.4 | async-start | bytes 1310720 | tf_op jit(solution)/shard_map/all_to_all | solution.py:82
  68.8 43.1 %all-to-all-start = ((bf16[32,34,256]{2,1,0:T(8,128)(2,1)}), bf16[32,34,256]{2,1,0:T(8,128)(2,1)S(1)}, u32[]{:S(2)}, u32[]{:S(2)}) async-start(bf16[32,34,256]{2,1,0:T(8,128)(2,1)} %bitcast.2), calls=%async_computation | async-start | bytes 1310720 | tf_op jit(solution)/shard_map/all_to_all | solution.py:67
  112.0 0.8 copy-start.2
  112.8 54.7 %all-to-all-start.2 = ((bf16[32,8,1792]{2,1,0:T(8,128)(2,1)}), bf16[32,8,1792]{2,1,0:T(8,128)(2,1)S(1)}, u32[]{:S(2)}, u32[]{:S(2)}) async-start(bf16[32,8,1792]{2,1,0:T(8,128)(2,1)} %bitcast.5), calls=%async_computation.2 | async-start | bytes 1835008 | tf_op jit(solution)/shard_map/all_to_all | solution.py:38
  167.6 54.8 %all-to-all-start.1 = ((bf16[32,8,1792]{2,1,0:T(8,128)(2,1)}), bf16[32,8,1792]{2,1,0:T(8,128)(2,1)S(1)}, u32[]{:S(2)}, u32[]{:S(2)}) async-start(bf16[32,8,1792]{2,1,0:T(8,128)(2,1)} %bitcast.3), calls=%async_computation.1 | async-start | bytes 1835008 | tf_op jit(solution)/shard_map/all_to_all | solution.py:37
  172.1 211.8 %all-reduce.4.cloned.1.call-start = ((), (), s32[]{:S(2)}) async-start(), calls=%async_computation.7 | async-start | bytes 15597568 | tf_op jit(solution)/shard_map/psum | solution.py:71
  390.5 66.6 %all-to-all-start.5 = ((bf16[16,112,1088]{2,1,0:T(8,128)(2,1)}), bf16[16,112,1088]{2,1,0:T(8,128)(2,1)}, u32[]{:S(2)}, u32[]{:S(2)}) async-start(bf16[16,112,1088]{2,1,0:T(8,128)(2,1)} %stack.2), calls=%async_computation.5 | async-start | bytes 8257536 | tf_op jit(solution)/shard_map/all_to_all | solution.py:96
  457.0 53.3 %all-to-all-start.3 = ((bf16[32,34,256]{2,1,0:T(8,128)(2,1)}), bf16[32,34,256]{2,1,0:T(8,128)(2,1)S(1)}, u32[]{:S(2)}, u32[]{:S(2)}) async-start(bf16[32,34,256]{2,1,0:T(8,128)(2,1)} %convolution_convert_fusion.5), calls=%async_computation.3 | async-start | bytes 1310720 | tf_op jit(solution)/shard_map/all_to_all | solution.py:75
  484.6 29.8 %copy-start.3 = (bf16[1088,256]{1,0:T(8,128)(2,1)S(1)}, bf16[1088,256]{1,0:T(8,128)(2,1)}, u32[]{:S(2)}) copy-start(bf16[1088,256]{1,0:T(8,128)(2,1)} %reshape.114) | copy-start | bytes 1671172
  510.3 43.1 %all-to-all-start.6 = ((bf16[32,34,256]{2,1,0:T(8,128)(2,1)}), bf16[32,34,256]{2,1,0:T(8,128)(2,1)S(1)}, u32[]{:S(2)}, u32[]{:S(2)}) async-start(bf16[32,34,256]{2,1,0:T(8,128)(2,1)} %convolution_convert_fusion.4), calls=%async_computation.6 | async-start | bytes 1310720 | tf_op jit(solution)/shard_map/all_to_all | solution.py:102
  520.1 34.7 %copy-start.1 = (bf16[128,256]{1,0:T(8,128)(2,1)S(1)}, bf16[128,256]{1,0:T(8,128)(2,1)}, u32[]{:S(2)}) copy-start(bf16[128,256]{1,0:T(8,128)(2,1)} %param.11) | copy-start | bytes 196612
Sparse Core Ops, SparseCore 0:
  225.6 158.2 all-reduce.3
